TPU v7x, 32 devices: a whole 2x2x4 slice. The times are simulated.
32 devices in a mesh: groups: 2 (over y), tensor: 4 (over z), section: 4 (over x, core).
Axes of the slice: x: 2, y: 2, z: 4, core: 2. Of those that a mesh axis runs over, the one named last changes fastest.
Arguments:
- inputs: bfloat16 [4, 64, 8192], P('groups', None, 'tensor'), parts along dimension 0, may hold values from -6 to 6
- gains: bfloat16 [4, 8192], P('section'), may hold values from 0.099609375 to 1.8984375
- keep_mask: int32 [4, 128, 128], P('section', 'tensor'), may hold values from 0 to 1, as said below
- block_values: bfloat16 [4, 12288, 4096], P('section', 'tensor'), may hold values from -0.09375 to 0.09375
- head: bfloat16 [32000, 8192], P(('tensor', 'section')), may hold values from -30 to 30
- targets: int32 [4, 64], P('groups'), parts along dimension 0, may hold values from 0 to 31999
Outputs:
- token_loss: float32 [4, 64], P('groups'), parts along dimension 0
- mean_loss: float32 [2], P('groups'), parts along dimension 0
There are 2 independent parts, one for each index of `groups`. A program takes and returns all parts, laid end to end along the dimension named above; an argument that names none is the same for every part. Nothing has to cross between parts.
Inputs may be any that keep to these rules, and one draw needn't show every extreme that they name: `keep_mask`: in each section, band t (block rows t * 32 to (t + 1) * 32 - 1) keeps between 1024 and 3072 blocks, and some band of each section keeps exactly 3072. List slots past a band's count of kept blocks are not read.
All inputs are finite; a program needn't handle non-finite values.
Results may differ from a plain program's by a relative error of at most 0.0044.
The roundings to bfloat16 on the way count: a program that leaves them out, or rounds other values in their place, can miss the bound.
Values may be sent and summed in bfloat16 or wider, within the bound.
A program may use at most 320 MiB of HBM per device.

v0:
```python
import jax
import jax.numpy as jnp
from jax import lax
from jax.sharding import PartitionSpec as P

D = 8192
BLK = 64
epsilon = 1e-05


def shifted(block, axis, distance):
    devices = range(lax.axis_size(axis))
    route = [(i - distance, i) for i in devices if i - distance in devices]
    return lax.ppermute(block, axis, route)


def from_root(block, axis, source):
    block = jnp.where(lax.axis_index(axis) == source, block, jnp.zeros_like(block))
    return lax.psum(block, axis)


def joined(value, axis, combine):
    everything = jax.tree.map(lambda part: lax.all_gather(part, axis), value)
    leading = jax.tree.map(lambda part: part[0], everything)

    def turn(k, so_far):
        return combine(so_far, jax.tree.map(lambda part: part[k], everything))

    return lax.fori_loop(1, lax.axis_size(axis), turn, leading)


def merge_parts(earlier, later):
    top = jnp.maximum(earlier[0], later[0])
    total = earlier[1] * jnp.exp(earlier[0] - top) + later[1] * jnp.exp(later[0] - top)
    return (top, total, earlier[2] + later[2])


def on_device(inputs, gains, keep_mask, block_values, head, targets):
    section_count = lax.axis_size("section")
    tensor_index = lax.axis_index("tensor")
    section_index = lax.axis_index("section")
    micro_count, row_count, local_width = inputs.shape
    band_rows, block_count = (keep_mask.shape[1], keep_mask.shape[2])
    flat_mask = keep_mask[0].reshape(-1)
    slots = jnp.clip(jnp.cumsum(flat_mask, dtype=jnp.int32) - 1, 0, block_values.shape[1] - 1)
    picked = block_values[0][slots] * flat_mask[:, None].astype(jnp.bfloat16)
    panel = (
        picked.reshape(band_rows, block_count, BLK, BLK)
        .transpose(0, 2, 1, 3)
        .reshape(band_rows * BLK, D)
    )
    gain_row = gains[0]
    column_panel = lax.all_to_all(panel, "tensor", split_axis=1, concat_axis=0, tiled=True)
    timesteps = micro_count + section_count - 1
    incoming = jnp.zeros((row_count, local_width), jnp.bfloat16)
    finished = [None] * micro_count
    for moment in range(timesteps):
        current = jnp.where(section_index == 0, inputs[min(moment, micro_count - 1)], incoming)
        apply_widened = lax.all_gather(current, "tensor", axis=1, tiled=True).astype(jnp.float32)
        scaled = (apply_widened * gain_row.astype(jnp.float32)).astype(jnp.bfloat16)
        projected = jnp.dot(scaled, column_panel, preferred_element_type=jnp.float32)
        projected, apply_sumsq = (projected, jnp.sum(apply_widened * apply_widened, axis=1))
        update = projected * lax.rsqrt(apply_sumsq[:, None] / D + epsilon)
        outgoing = (current.astype(jnp.float32) + update).astype(jnp.bfloat16)
        done_index = moment - (section_count - 1)
        if 0 <= done_index < micro_count:
            finished[done_index] = outgoing
        if moment < timesteps - 1:
            incoming = shifted(outgoing, "section", 1)
    final_rows = jnp.stack(finished).reshape(micro_count * row_count, local_width)
    vocab_rows = head.shape[0]
    relayed = from_root(final_rows, "section", section_count - 1)
    portion = lax.all_gather(relayed, "tensor", axis=1, tiled=True)
    raw_logits = lax.dot_general(
        portion, head, (((1,), (1,)), ((), ())), preferred_element_type=jnp.float32
    )
    widened = portion.astype(jnp.float32)
    raw_logits, final_sumsq = (raw_logits, jnp.sum(widened * widened, axis=1))
    logits = raw_logits * lax.rsqrt(final_sumsq[:, None] / D + epsilon)
    vocab_start = (tensor_index * section_count + section_index) * vocab_rows
    local_ids = targets.reshape(-1) - vocab_start
    matches = jnp.arange(vocab_rows, dtype=jnp.int32)[None, :] == local_ids[:, None]
    target_logit = jnp.sum(jnp.where(matches, logits, 0.0), axis=1)
    local_top = jnp.max(logits, axis=1)
    local_total = jnp.sum(jnp.exp(logits - local_top[:, None]), axis=1)
    top, total, chosen = joined(
        (local_top, local_total, target_logit), ("tensor", "section"), merge_parts
    )
    token_loss = (top + jnp.log(total) - chosen).reshape(micro_count, row_count)
    mean_loss = jnp.mean(token_loss).reshape(1)
    return (token_loss, mean_loss)


def solution(mesh):
    placed = (
        P("groups", None, "tensor"),
        P("section", None),
        P("section", "tensor", None),
        P("section", "tensor", None),
        P(("tensor", "section"), None),
        P("groups", None),
    )
    return jax.shard_map(
        on_device,
        mesh=mesh,
        in_specs=placed,
        out_specs=(P("groups", None), P("groups")),
        check_vma=False,
    )
```

profile of v0, /device:TPU:0, one launch (start us, length us, event | category | flops | bytes accessed | tf_op | source)
XLA Modules:
  0.0 1553.3 jit_solution(10972753995354582155)
XLA Ops:
  7.2 0.7 bitcast_convert_fusion
  7.9 1.0 reduce-window.9
  9.3 67.2 %gather_fusion = bf16[4096,4096]{1,0:T(8,128)(2,1)} fusion(bf16[3072,4096]{1,0:T(8,128)(2,1)} %bitcast.77, s32[4096]{0:T(1024)S(1)} %broadcast_clamp_fusion), kind=kCustom, calls=%fused_computation | custom fusion | bytes 67125248 | tf_op jit(solution)/shard_map/gather | solution.py:46
  76.4 41.0 %copy.11 = bf16[4096,4096]{0,1:T(8,128)(2,1)} copy(bf16[4096,4096]{1,0:T(8,128)(2,1)} %gather_fusion) | data formatting | bytes 67108864 | tf_op jit(solution)/shard_map/gather | solution.py:46
  117.4 23.1 %copy.14 = bf16[512,8,32,128]{3,2,1,0:T(8,128)(2,1)} copy(bf16[512,8,32,128]{3,1,2,0:T(8,128)(2,1)} %bitcast.84) | data formatting | bytes 67108864
  140.5 23.1 %multiply_bitcast_fusion = bf16[32,64,128,64]{2,0,3,1:T(8,128)(2,1)} fusion(bf16[32,128,64,64]{1,0,3,2:T(8,128)(2,1)} %bitcast.83, bf16[32,128]{1,0:T(8,128)(2,1)S(1)} %bitcast_convert_fusion), kind=kLoop, calls=%fused_computation.11 | loop fusion | flops 16777216 | bytes 67117056 | tf_op jit(solution)/shard_map/transpose | solution.py:49
  163.6 110.4 %copy.12 = bf16[32,64,128,64]{1,0,3,2:T(8,128)(2,1)} copy(bf16[32,64,128,64]{2,0,3,1:T(8,128)(2,1)} %multiply_bitcast_fusion) | data formatting | bytes 67108864 | tf_op jit(solution)/shard_map/transpose | solution.py:49
  274.0 90.3 %all_to_all.14 = bf16[2048,4,2048]{0,2,1:T(8,128)(2,1)} reshape(bf16[32,64,128,64]{1,0,3,2:T(8,128)(2,1)} %copy.12) | data formatting | bytes 67108864 | tf_op jit(solution)/shard_map/all_to_all | solution.py:53
  364.4 9.8 all-to-all-start
  374.3 0.7 slice_select_fusion
  375.6 210.2 %all-gather.24.cloned.1.call-done = bf16[1,64,8192]{2,1,0:T(8,128)(2,1)} async-done(((bf16[1,64,2048]{2,1,0:T(8,128)(2,1)}), bf16[1,64,8192]{2,1,0:T(8,128)(2,1)}) %all-gather.24.cloned.1.call-update) | async-done | bytes 1048592 | tf_op jit(solution)/shard_map/all_gather | solution.py:59
  585.8 1.5 fusion.18
  587.4 527.8 %all-to-all-done = bf16[2048,4,2048]{0,2,1:T(8,128)(2,1)} async-done(((bf16[2048,4,2048]{0,2,1:T(8,128)(2,1)}), bf16[2048,4,2048]{0,2,1:T(8,128)(2,1)}, u32[]{:S(2)}, u32[]{:S(2)}) %all-to-all-start) | async-done | bytes 33554464 | tf_op jit(solution)/shard_map/all_to_all | solution.py:53
  1115.1 42.8 %copy.13 = bf16[4,2048,2048]{2,1,0:T(8,128)(2,1)} copy(bf16[4,2048,2048]{1,2,0:T(8,128)(2,1)} %bitcast.12) | data formatting | bytes 67108864 | tf_op jit(solution)/shard_map/all_to_all | solution.py:53
  1157.9 13.7 fusion.8
  1171.7 1.3 collective-permute-start
  1173.0 1.1 collective-permute-done
  1174.1 0.7 bitcast_select_fusion.3
  1174.9 32.4 %all-gather.14.cloned.1.call-done = bf16[64,8192]{1,0:T(8,128)(2,1)} async-done(((bf16[64,2048]{1,0:T(8,128)(2,1)}), bf16[64,8192]{1,0:T(8,128)(2,1)}) %all-gather.14.cloned.1.call-update) | async-done | bytes 1048592 | tf_op jit(solution)/shard_map/all_gather | solution.py:59
  1207.3 1.5 fusion.10
  1208.9 16.8 %add_convert_fusion.3 = bf16[64,2048]{1,0:T(8,128)(2,1)S(1)} fusion(bf16[64,2048]{1,0:T(8,128)(2,1)} %bitcast_select_fusion.3, f32[64]{0:T(128)S(1)} %add_rsqrt_fusion.4, bf16[8192,2048]{1,0:T(8,128)(2,1)} %bitcast.79, bf16[64,8192]{1,0:T(8,128)(2,1)} %all-gather.14.cloned.1.call-done, f32[8192]{0:T(1024)S(1)} %bitcast.86), kind=kOutput, calls=%fused_computation.54 | convolution fusion | flops 2149580800 | bytes 35160320 | tf_op jit(solution)/shard_map/dot_general | solution.py:61
  1225.7 1.6 collective-permute-start.1
  1227.3 1.1 collective-permute-done.1
  1228.4 0.7 bitcast_select_fusion.2
  1229.4 32.3 %all-gather.16.cloned.1.call-done = bf16[64,8192]{1,0:T(8,128)(2,1)} async-done(((bf16[64,2048]{1,0:T(8,128)(2,1)}), bf16[64,8192]{1,0:T(8,128)(2,1)}) %all-gather.16.cloned.1.call-update) | async-done | bytes 1048592 | tf_op jit(solution)/shard_map/all_gather | solution.py:59
  1261.7 1.5 fusion.12
  1263.2 16.8 %add_convert_fusion.2 = bf16[64,2048]{1,0:T(8,128)(2,1)S(1)} fusion(bf16[64,2048]{1,0:T(8,128)(2,1)} %bitcast_select_fusion.2, f32[64]{0:T(128)S(1)} %add_rsqrt_fusion.3, bf16[8192,2048]{1,0:T(8,128)(2,1)} %bitcast.80, bf16[64,8192]{1,0:T(8,128)(2,1)} %all-gather.16.cloned.1.call-done, f32[8192]{0:T(1024)S(1)} %bitcast.87), kind=kOutput, calls=%fused_computation.53 | convolution fusion | flops 2149580800 | bytes 35160320 | tf_op jit(solution)/shard_map/dot_general | solution.py:61
  1280.0 1.6 collective-permute-start.2
  1281.7 1.1 collective-permute-done.2
  1282.8 0.7 bitcast_select_fusion.1
  1283.6 32.5 %all-gather.18.cloned.1.call-done = bf16[64,8192]{1,0:T(8,128)(2,1)} async-done(((bf16[64,2048]{1,0:T(8,128)(2,1)}), bf16[64,8192]{1,0:T(8,128)(2,1)}) %all-gather.18.cloned.1.call-update) | async-done | bytes 1048592 | tf_op jit(solution)/shard_map/all_gather | solution.py:59
  1316.1 1.5 fusion.14
  1317.6 16.8 %add_convert_fusion.1 = bf16[64,2048]{1,0:T(8,128)(2,1)S(1)} fusion(bf16[64,2048]{1,0:T(8,128)(2,1)} %bitcast_select_fusion.1, f32[64]{0:T(128)S(1)} %add_rsqrt_fusion.2, bf16[8192,2048]{1,0:T(8,128)(2,1)} %bitcast.81, bf16[64,8192]{1,0:T(8,128)(2,1)} %all-gather.18.cloned.1.call-done, f32[8192]{0:T(1024)S(1)} %bitcast.88), kind=kOutput, calls=%fused_computation.52 | convolution fusion | flops 2149580800 | bytes 35160320 | tf_op jit(solution)/shard_map/dot_general | solution.py:61
  1334.4 1.6 collective-permute-start.3
  1336.0 1.1 collective-permute-done.3
  1337.2 0.7 bitcast_select_fusion
  1338.2 32.3 %all-gather.20.cloned.1.call-done = bf16[64,8192]{1,0:T(8,128)(2,1)} async-done(((bf16[64,2048]{1,0:T(8,128)(2,1)}), bf16[64,8192]{1,0:T(8,128)(2,1)}) %all-gather.20.cloned.1.call-update) | async-done | bytes 1048592 | tf_op jit(solution)/shard_map/all_gather | solution.py:59
  1370.4 1.5 fusion.16
  1372.0 16.8 %fusion.30 = bf16[1,64,2048]{2,1,0:T(8,128)(2,1)S(1)} fusion(bf16[64,2048]{1,0:T(8,128)(2,1)} %bitcast_select_fusion, f32[64]{0:T(128)S(1)} %add_rsqrt_fusion.1, bf16[8192,2048]{1,0:T(8,128)(2,1)} %bitcast.82, bf16[64,8192]{1,0:T(8,128)(2,1)} %all-gather.20.cloned.1.call-done, f32[8192]{0:T(1024)S(1)} %bitcast.89), kind=kOutput, calls=%fused_computation.55 | convolution fusion | flops 2149580800 | bytes 35160320 | tf_op jit(solution)/shard_map/dot_general | solution.py:61
  1388.8 0.9 maximum_select_fusion
  1389.7 32.8 %all-reduce.2.cloned.1.call-done = bf16[128,2048]{1,0:T(8,128)(2,1)} async-done(((bf16[128,2048]{1,0:T(8,128)(2,1)}), bf16[128,2048]{1,0:T(8,128)(2,1)}) %all-reduce.2.cloned.1.call-update) | async-done | bytes 524304 | tf_op jit(solution)/shard_map/psum | solution.py:19
  1422.7 47.4 %all-gather.22.cloned.1.call-done = bf16[128,8192]{1,0:T(8,128)(2,1)} async-done(((bf16[128,2048]{1,0:T(8,128)(2,1)}), bf16[128,8192]{1,0:T(8,128)(2,1)}) %all-gather.22.cloned.1.call-update) | async-done | bytes 2097168 | tf_op jit(solution)/shard_map/all_gather | solution.py:73
  1470.1 2.1 multiply_reduce_fusion
  1472.2 15.0 fusion.41
  1487.3 19.0 %all-gather.4 = f32[16,1,128]{2,1,0:T(1,128)S(1)} all-gather(f32[1,1,128]{2,1,0:T(1,128)S(1)} %bitcast.98), channel_id=3, replica_groups=mesh['groups'=2,'tensor'=4,'section'=4] {'tensor','section'}, dimensions={0}, use_global_device_ids=true | all-gather | bytes 8704 | tf_op jit(solution)/shard_map/all_gather | solution.py:23
  1506.6 17.3 %all-gather.5 = f32[16,1,128]{2,1,0:T(1,128)S(1)} all-gather(f32[1,1,128]{2,1,0:T(1,128)S(1)} %bitcast.100), channel_id=4, replica_groups=mesh['groups'=2,'tensor'=4,'section'=4] {'tensor','section'}, dimensions={0}, use_global_device_ids=true | all-gather | bytes 8704 | tf_op jit(solution)/shard_map/all_gather | solution.py:23
  1523.9 18.7 %all-gather.6 = f32[16,1,128]{2,1,0:T(1,128)S(1)} all-gather(f32[1,1,128]{2,1,0:T(1,128)S(1)} %bitcast.99), channel_id=5, replica_groups=mesh['groups'=2,'tensor'=4,'section'=4] {'tensor','section'}, dimensions={0}, use_global_device_ids=true | all-gather | bytes 8704 | tf_op jit(solution)/shard_map/all_gather | solution.py:23
  1542.6 0.7 while.19
  (60 shorter events, 3.8 us)
Async XLA Ops:
  364.3 9.9 copy-start.1
  364.3 11.2 copy-start.3
  364.4 750.8 %all-to-all-start = ((bf16[2048,4,2048]{0,2,1:T(8,128)(2,1)}), bf16[2048,4,2048]{0,2,1:T(8,128)(2,1)}, u32[]{:S(2)}, u32[]{:S(2)}) async-start(bf16[2048,4,2048]{0,2,1:T(8,128)(2,1)} %all_to_all.14), calls=%async_computation | async-start | bytes 67108864 | tf_op jit(solution)/shard_map/all_to_all | solution.py:53
  374.2 211.6 %all-gather.24.cloned.1.call-start = ((), (), s32[]{:S(2)}) async-start(), calls=%async_computation.7 | async-start | bytes 1310720 | tf_op jit(solution)/shard_map/all_gather | solution.py:59
  375.0 832.3 %all-gather.14.cloned.1.call-start = ((), (), s32[]{:S(2)}) async-start(), calls=%async_computation.1 | async-start | bytes 1310720 | tf_op jit(solution)/shard_map/all_gather | solution.py:59
  1115.1 42.8 %copy-start = (bf16[1,64,8192]{2,1,0:T(8,128)(2,1)S(1)}, bf16[1,64,8192]{2,1,0:T(8,128)(2,1)}, u32[]{:S(2)}) copy-start(bf16[1,64,8192]{2,1,0:T(8,128)(2,1)} %all-gather.24.cloned.1.call-done) | copy-start | bytes 3145732
  1115.1 42.8 %copy-start.2 = (bf16[1,64,2048]{2,1,0:T(8,128)(2,1)S(1)}, bf16[1,64,2048]{2,1,0:T(8,128)(2,1)}, u32[]{:S(2)}) copy-start(bf16[1,64,2048]{2,1,0:T(8,128)(2,1)} %slice_select_fusion) | copy-start | bytes 786436
  1171.7 2.4 collective-permute-start
  1174.8 86.8 %all-gather.16.cloned.1.call-start = ((), (), s32[]{:S(2)}) async-start(), calls=%async_computation.2 | async-start | bytes 1310720 | tf_op jit(solution)/shard_map/all_gather | solution.py:59
  1225.7 2.8 collective-permute-start.1
  1229.2 86.9 %all-gather.18.cloned.1.call-start = ((), (), s32[]{:S(2)}) async-start(), calls=%async_computation.3 | async-start | bytes 1310720 | tf_op jit(solution)/shard_map/all_gather | solution.py:59
  1280.0 2.8 collective-permute-start.2
  1283.5 86.9 %all-gather.20.cloned.1.call-start = ((), (), s32[]{:S(2)}) async-start(), calls=%async_computation.4 | async-start | bytes 1310720 | tf_op jit(solution)/shard_map/all_gather | solution.py:59
  1334.4 88.2 %copy-start.4 = (s32[2,64]{1,0:T(2,128)S(1)}, s32[2,64]{1,0:T(2,128)}, u32[]{:S(2)}) copy-start(s32[2,64]{1,0:T(2,128)} %param.13) | copy-start | bytes 1540
  1334.4 2.8 collective-permute-start.3
  1337.9 84.6 %all-reduce.2.cloned.1.call-start = ((), (), s32[]{:S(2)}) async-start(), calls=%async_computation.5 | async-start | bytes 1048576 | tf_op jit(solution)/shard_map/psum | solution.py:19
  1389.7 80.4 %all-gather.22.cloned.1.call-start = ((), (), s32[]{:S(2)}) async-start(), calls=%async_computation.6 | async-start | bytes 2621440 | tf_op jit(solution)/shard_map/all_gather | solution.py:73
Sparse Core Ops, SparseCore 0:
  376.6 209.1 all-gather.23
  1175.0 32.3 all-gather.13
  1229.3 32.3 all-gather.15
  1283.7 32.3 all-gather.17
  1338.0 32.3 all-gather.19
  1389.8 32.7 all-reduce.1
  1424.1 45.9 all-gather.21
where the time goes:
time: 1570 us; the launch traced here: 1550 us
  waiting for transfers between devices  952 us (61%)
  local copies, waits for them, and re-layouts  376 us (24%)
  matrix products  95.9 us (6%)
  blocking collectives  55 us (4%)
  other arithmetic  40.6 us (3%)
  starting transfers between devices  17.1 us (1%)
  between operations  16.4 us (1%)
    all_to_all x1, waiting for transfers between devices, on_device(): lax.all_to_all(panel, 'tensor', split_axis=1, concat_axis=0, tiled=True)  528 us
    all_gather x5, waiting for transfers between devices, on_device(): lax.all_gather(current, 'tensor', axis=1, tiled=True).astype(jnp.float32)  340 us
    all_to_all x2, local copies, waits for them, and re-layouts, on_device(): lax.all_to_all(panel, 'tensor', split_axis=1, concat_axis=0, tiled=True)  133 us
    transpose x1, local copies, waits for them, and re-layouts, on_device(): panel = picked.reshape(band_rows, block_count, BLK, BLK).transpose(0, 2,...  110 us
    gather x2, local copies, waits for them, and re-layouts, on_device(): picked = block_values[0][slots] * flat_mask[:, None].astype(jnp.bfloat16)  108 us
    dot_general x5, matrix products, on_device(): jnp.dot(scaled, column_panel, preferred_element_type=jnp.float32)  80.9 us
    all_gather x3, blocking collectives, joined(): everything = jax.tree.map(lambda part: lax.all_gather(part, axis), value)  55 us
    all_gather x1, waiting for transfers between devices, on_device(): portion = lax.all_gather(relayed, 'tensor', axis=1, tiled=True)  47.4 us
  transfers between devices with their start and end apart: 12, of which 12 were waited for; matrix products, arithmetic and copies ran while one was open for 0% of the time, Pallas kernels for 0%

commit v1 on v0

--- a/solution.py
+++ b/solution.py
@@ -70,7 +70,16 @@
     final_rows = jnp.stack(finished).reshape(micro_count * row_count, local_width)
     vocab_rows = head.shape[0]
     relayed = from_root(final_rows, "section", section_count - 1)
-    portion = lax.all_gather(relayed, "tensor", axis=1, tiled=True)
+    ways = lax.axis_size("tensor")
+    up = [(d, (d + 1) % ways) for d in range(ways)]
+    down = [(d, (d - 1) % ways) for d in range(ways)]
+    earlier_2, later_2 = ([relayed], [relayed])
+    for _ in range(ways // 2):
+        earlier_2.append(lax.ppermute(earlier_2[-1], "tensor", up))
+    for _ in range((ways - 1) // 2):
+        later_2.append(lax.ppermute(later_2[-1], "tensor", down))
+    line = jnp.concatenate([*earlier_2[::-1], *later_2[1:]], axis=1)
+    portion = jnp.roll(line, (lax.axis_index("tensor") - ways // 2) * relayed.shape[1], axis=1)
     raw_logits = lax.dot_general(
         portion, head, (((1,), (1,)), ((), ())), preferred_element_type=jnp.float32
     )

time: 1570 us -> 1550 us (0.987)
  waiting for transfers between devices: 952 us -> 936 us
    all_gather x1 -> x0, waiting for transfers between devices: 47.4 us -> none  [on_device(): portion = lax.all_gather(relayed, 'tensor', axis=1, tiled=True)]
    ppermute x0 -> x3, waiting for transfers between devices: none -> 31.2 us  [the longest x2 25.9 us: on_device(): earlier_2.append(lax.ppermute(earlier_2[-1], 'tensor', up))]
  transfers between devices with their start and end apart: 12 -> 14, of which waited for: 12 -> 14; matrix products, arithmetic and copies ran while one was open for 0% -> 0% of each run, Pallas kernels for 0% -> 0%
where the time goes in v1:
time: 1550 us; the launch traced here: 1540 us
  waiting for transfers between devices  936 us (60%)
  local copies, waits for them, and re-layouts  377 us (24%)
  matrix products  95.3 us (6%)
  blocking collectives  55.6 us (4%)
  other arithmetic  39 us (3%)
  starting transfers between devices  22.4 us (1%)
  between operations  16.4 us (1%)
    all_to_all x1, waiting for transfers between devices, on_device(): lax.all_to_all(panel, 'tensor', split_axis=1, concat_axis=0, tiled=True)  528 us
    all_gather x5, waiting for transfers between devices, on_device(): lax.all_gather(current, 'tensor', axis=1, tiled=True).astype(jnp.float32)  340 us
    all_to_all x2, local copies, waits for them, and re-layouts, on_device(): lax.all_to_all(panel, 'tensor', split_axis=1, concat_axis=0, tiled=True)  133 us
    transpose x1, local copies, waits for them, and re-layouts, on_device(): panel = picked.reshape(band_rows, block_count, BLK, BLK).transpose(0, 2,...  110 us
    gather x2, local copies, waits for them, and re-layouts, on_device(): picked = block_values[0][slots] * flat_mask[:, None].astype(jnp.bfloat16)  108 us
    dot_general x5, matrix products, on_device(): jnp.dot(scaled, column_panel, preferred_element_type=jnp.float32)  80.9 us
    all_gather x3, blocking collectives, joined(): everything = jax.tree.map(lambda part: lax.all_gather(part, axis), value)  55.6 us
    psum x1, waiting for transfers between devices, from_root(): return lax.psum(block, axis)  32.9 us
  transfers between devices with their start and end apart: 14, of which 14 were waited for; matrix products, arithmetic and copies ran while one was open for 0% of the time, Pallas kernels for 0%

profile of v1, /device:TPU:0, one launch (start us, length us, event | category | flops | bytes accessed | tf_op | source)
XLA Modules:
  0.0 1542.2 jit_solution(6049712685755973413)
XLA Ops:
  7.2 0.7 bitcast_convert_fusion
  7.9 1.0 reduce-window.9
  9.3 67.2 %gather_fusion = bf16[4096,4096]{1,0:T(8,128)(2,1)} fusion(bf16[3072,4096]{1,0:T(8,128)(2,1)} %bitcast.76, s32[4096]{0:T(1024)S(1)} %broadcast_clamp_fusion), kind=kCustom, calls=%fused_computation | custom fusion | bytes 67125248 | tf_op jit(solution)/shard_map/gather | solution.py:46
  76.4 41.0 %copy.11 = bf16[4096,4096]{0,1:T(8,128)(2,1)} copy(bf16[4096,4096]{1,0:T(8,128)(2,1)} %gather_fusion) | data formatting | bytes 67108864 | tf_op jit(solution)/shard_map/gather | solution.py:46
  117.4 23.1 %copy.14 = bf16[512,8,32,128]{3,2,1,0:T(8,128)(2,1)} copy(bf16[512,8,32,128]{3,1,2,0:T(8,128)(2,1)} %bitcast.83) | data formatting | bytes 67108864
  140.5 23.1 %multiply_bitcast_fusion = bf16[32,64,128,64]{2,0,3,1:T(8,128)(2,1)} fusion(bf16[32,128,64,64]{1,0,3,2:T(8,128)(2,1)} %bitcast.82, bf16[32,128]{1,0:T(8,128)(2,1)S(1)} %bitcast_convert_fusion), kind=kLoop, calls=%fused_computation.11 | loop fusion | flops 16777216 | bytes 67117056 | tf_op jit(solution)/shard_map/transpose | solution.py:49
  163.6 110.4 %copy.12 = bf16[32,64,128,64]{1,0,3,2:T(8,128)(2,1)} copy(bf16[32,64,128,64]{2,0,3,1:T(8,128)(2,1)} %multiply_bitcast_fusion) | data formatting | bytes 67108864 | tf_op jit(solution)/shard_map/transpose | solution.py:49
  274.0 90.3 %all_to_all.14 = bf16[2048,4,2048]{0,2,1:T(8,128)(2,1)} reshape(bf16[32,64,128,64]{1,0,3,2:T(8,128)(2,1)} %copy.12) | data formatting | bytes 67108864 | tf_op jit(solution)/shard_map/all_to_all | solution.py:53
  364.4 9.8 all-to-all-start
  375.6 210.2 %all-gather.21.cloned.1.call-done = bf16[1,64,8192]{2,1,0:T(8,128)(2,1)} async-done(((bf16[1,64,2048]{2,1,0:T(8,128)(2,1)}), bf16[1,64,8192]{2,1,0:T(8,128)(2,1)}) %all-gather.21.cloned.1.call-update) | async-done | bytes 1048592 | tf_op jit(solution)/shard_map/all_gather | solution.py:59
  585.8 1.5 fusion.18
  587.4 527.8 %all-to-all-done = bf16[2048,4,2048]{0,2,1:T(8,128)(2,1)} async-done(((bf16[2048,4,2048]{0,2,1:T(8,128)(2,1)}), bf16[2048,4,2048]{0,2,1:T(8,128)(2,1)}, u32[]{:S(2)}, u32[]{:S(2)}) %all-to-all-start) | async-done | bytes 33554464 | tf_op jit(solution)/shard_map/all_to_all | solution.py:53
  1115.1 42.8 %copy.13 = bf16[4,2048,2048]{2,1,0:T(8,128)(2,1)} copy(bf16[4,2048,2048]{1,2,0:T(8,128)(2,1)} %bitcast.12) | data formatting | bytes 67108864 | tf_op jit(solution)/shard_map/all_to_all | solution.py:53
  1157.9 13.7 fusion.8
  1171.7 1.3 collective-permute-start
  1173.0 1.1 collective-permute-done
  1174.1 0.7 bitcast_select_fusion.3
  1174.9 32.4 %all-gather.13.cloned.1.call-done = bf16[64,8192]{1,0:T(8,128)(2,1)} async-done(((bf16[64,2048]{1,0:T(8,128)(2,1)}), bf16[64,8192]{1,0:T(8,128)(2,1)}) %all-gather.13.cloned.1.call-update) | async-done | bytes 1048592 | tf_op jit(solution)/shard_map/all_gather | solution.py:59
  1207.3 1.5 fusion.10
  1208.9 16.8 %add_convert_fusion.3 = bf16[64,2048]{1,0:T(8,128)(2,1)S(1)} fusion(bf16[64,2048]{1,0:T(8,128)(2,1)} %bitcast_select_fusion.3, f32[64]{0:T(128)S(1)} %add_rsqrt_fusion.4, bf16[8192,2048]{1,0:T(8,128)(2,1)} %bitcast.78, bf16[64,8192]{1,0:T(8,128)(2,1)} %all-gather.13.cloned.1.call-done, f32[8192]{0:T(1024)S(1)} %bitcast.85), kind=kOutput, calls=%fused_computation.55 | convolution fusion | flops 2149580800 | bytes 35160320 | tf_op jit(solution)/shard_map/dot_general | solution.py:61
  1225.7 1.6 collective-permute-start.1
  1227.3 1.1 collective-permute-done.1
  1228.4 0.7 bitcast_select_fusion.2
  1229.4 32.3 %all-gather.15.cloned.1.call-done = bf16[64,8192]{1,0:T(8,128)(2,1)} async-done(((bf16[64,2048]{1,0:T(8,128)(2,1)}), bf16[64,8192]{1,0:T(8,128)(2,1)}) %all-gather.15.cloned.1.call-update) | async-done | bytes 1048592 | tf_op jit(solution)/shard_map/all_gather | solution.py:59
  1261.7 1.5 fusion.12
  1263.2 16.8 %add_convert_fusion.2 = bf16[64,2048]{1,0:T(8,128)(2,1)S(1)} fusion(bf16[64,2048]{1,0:T(8,128)(2,1)} %bitcast_select_fusion.2, f32[64]{0:T(128)S(1)} %add_rsqrt_fusion.3, bf16[8192,2048]{1,0:T(8,128)(2,1)} %bitcast.79, bf16[64,8192]{1,0:T(8,128)(2,1)} %all-gather.15.cloned.1.call-done, f32[8192]{0:T(1024)S(1)} %bitcast.86), kind=kOutput, calls=%fused_computation.54 | convolution fusion | flops 2149580800 | bytes 35160320 | tf_op jit(solution)/shard_map/dot_general | solution.py:61
  1280.0 1.6 collective-permute-start.2
  1281.7 1.1 collective-permute-done.2
  1283.6 32.5 %all-gather.17.cloned.1.call-done = bf16[64,8192]{1,0:T(8,128)(2,1)} async-done(((bf16[64,2048]{1,0:T(8,128)(2,1)}), bf16[64,8192]{1,0:T(8,128)(2,1)}) %all-gather.17.cloned.1.call-update) | async-done | bytes 1048592 | tf_op jit(solution)/shard_map/all_gather | solution.py:59
  1316.1 1.5 fusion.14
  1317.6 16.8 %add_convert_fusion.1 = bf16[64,2048]{1,0:T(8,128)(2,1)S(1)} fusion(bf16[64,2048]{1,0:T(8,128)(2,1)} %bitcast_select_fusion.1, f32[64]{0:T(128)S(1)} %add_rsqrt_fusion.2, bf16[8192,2048]{1,0:T(8,128)(2,1)} %bitcast.80, bf16[64,8192]{1,0:T(8,128)(2,1)} %all-gather.17.cloned.1.call-done, f32[8192]{0:T(1024)S(1)} %bitcast.87), kind=kOutput, calls=%fused_computation.53 | convolution fusion | flops 2149580800 | bytes 35160320 | tf_op jit(solution)/shard_map/dot_general | solution.py:61
  1334.4 1.6 collective-permute-start.3
  1336.0 1.1 collective-permute-done.3
  1338.2 32.3 %all-gather.19.cloned.1.call-done = bf16[64,8192]{1,0:T(8,128)(2,1)} async-done(((bf16[64,2048]{1,0:T(8,128)(2,1)}), bf16[64,8192]{1,0:T(8,128)(2,1)}) %all-gather.19.cloned.1.call-update) | async-done | bytes 1048592 | tf_op jit(solution)/shard_map/all_gather | solution.py:59
  1370.4 1.5 fusion.16
  1372.0 16.8 %fusion.31 = bf16[1,64,2048]{2,1,0:T(8,128)(2,1)S(1)} fusion(bf16[64,2048]{1,0:T(8,128)(2,1)} %bitcast_select_fusion, f32[64]{0:T(128)S(1)} %add_rsqrt_fusion.1, bf16[8192,2048]{1,0:T(8,128)(2,1)} %bitcast.81, bf16[64,8192]{1,0:T(8,128)(2,1)} %all-gather.19.cloned.1.call-done, f32[8192]{0:T(1024)S(1)} %bitcast.88), kind=kOutput, calls=%fused_computation.56 | convolution fusion | flops 2149580800 | bytes 35160320 | tf_op jit(solution)/shard_map/dot_general | solution.py:61
  1388.8 0.9 maximum_select_fusion
  1389.7 32.9 %all-reduce.2.cloned.1.call-done = bf16[128,2048]{1,0:T(8,128)(2,1)} async-done(((bf16[128,2048]{1,0:T(8,128)(2,1)}), bf16[128,2048]{1,0:T(8,128)(2,1)}) %all-reduce.2.cloned.1.call-update) | async-done | bytes 524304 | tf_op jit(solution)/shard_map/psum | solution.py:19
  1422.6 1.5 collective-permute-start.4
  1424.0 13.1 collective-permute-done.4
  1437.2 3.8 collective-permute-start.6
  1441.1 12.7 collective-permute-done.5
  1453.9 1.1 constant_dynamic-update-slice_fusion.5
  1455.0 5.4 collective-permute-done.6
  1461.1 14.5 fusion.43
  1475.6 19.6 %all-gather.4 = f32[16,1,128]{2,1,0:T(1,128)S(1)} all-gather(f32[1,1,128]{2,1,0:T(1,128)S(1)} %bitcast.97), channel_id=3, replica_groups=mesh['groups'=2,'tensor'=4,'section'=4] {'tensor','section'}, dimensions={0}, use_global_device_ids=true | all-gather | bytes 8704 | tf_op jit(solution)/shard_map/all_gather | solution.py:23
  1495.5 17.3 %all-gather.5 = f32[16,1,128]{2,1,0:T(1,128)S(1)} all-gather(f32[1,1,128]{2,1,0:T(1,128)S(1)} %bitcast.99), channel_id=4, replica_groups=mesh['groups'=2,'tensor'=4,'section'=4] {'tensor','section'}, dimensions={0}, use_global_device_ids=true | all-gather | bytes 8704 | tf_op jit(solution)/shard_map/all_gather | solution.py:23
  1512.8 18.7 %all-gather.6 = f32[16,1,128]{2,1,0:T(1,128)S(1)} all-gather(f32[1,1,128]{2,1,0:T(1,128)S(1)} %bitcast.98), channel_id=5, replica_groups=mesh['groups'=2,'tensor'=4,'section'=4] {'tensor','section'}, dimensions={0}, use_global_device_ids=true | all-gather | bytes 8704 | tf_op jit(solution)/shard_map/all_gather | solution.py:23
  (73 shorter events, 7.3 us)
Async XLA Ops:
  364.3 9.9 copy-start.1
  364.3 11.2 copy-start.4
  364.4 750.8 %all-to-all-start = ((bf16[2048,4,2048]{0,2,1:T(8,128)(2,1)}), bf16[2048,4,2048]{0,2,1:T(8,128)(2,1)}, u32[]{:S(2)}, u32[]{:S(2)}) async-start(bf16[2048,4,2048]{0,2,1:T(8,128)(2,1)} %all_to_all.14), calls=%async_computation | async-start | bytes 67108864 | tf_op jit(solution)/shard_map/all_to_all | solution.py:53
  374.2 211.6 %all-gather.21.cloned.1.call-start = ((), (), s32[]{:S(2)}) async-start(), calls=%async_computation.6 | async-start | bytes 1310720 | tf_op jit(solution)/shard_map/all_gather | solution.py:59
  375.0 832.3 %all-gather.13.cloned.1.call-start = ((), (), s32[]{:S(2)}) async-start(), calls=%async_computation.1 | async-start | bytes 1310720 | tf_op jit(solution)/shard_map/all_gather | solution.py:59
  1115.1 42.8 %copy-start = (bf16[1,64,8192]{2,1,0:T(8,128)(2,1)S(1)}, bf16[1,64,8192]{2,1,0:T(8,128)(2,1)}, u32[]{:S(2)}) copy-start(bf16[1,64,8192]{2,1,0:T(8,128)(2,1)} %all-gather.21.cloned.1.call-done) | copy-start | bytes 3145732
  1115.1 42.8 %copy-start.2 = (bf16[1,64,2048]{2,1,0:T(8,128)(2,1)S(1)}, bf16[1,64,2048]{2,1,0:T(8,128)(2,1)}, u32[]{:S(2)}) copy-start(bf16[1,64,2048]{2,1,0:T(8,128)(2,1)} %slice_select_fusion) | copy-start | bytes 786436
  1171.7 2.4 collective-permute-start
  1174.8 86.8 %all-gather.15.cloned.1.call-start = ((), (), s32[]{:S(2)}) async-start(), calls=%async_computation.2 | async-start | bytes 1310720 | tf_op jit(solution)/shard_map/all_gather | solution.py:59
  1225.7 2.8 collective-permute-start.1
  1229.2 86.9 %all-gather.17.cloned.1.call-start = ((), (), s32[]{:S(2)}) async-start(), calls=%async_computation.3 | async-start | bytes 1310720 | tf_op jit(solution)/shard_map/all_gather | solution.py:59
  1280.0 2.8 collective-permute-start.2
  1283.5 86.9 %all-gather.19.cloned.1.call-start = ((), (), s32[]{:S(2)}) async-start(), calls=%async_computation.4 | async-start | bytes 1310720 | tf_op jit(solution)/shard_map/all_gather | solution.py:59
  1334.4 2.8 collective-permute-start.3
  1337.9 84.6 %all-reduce.2.cloned.1.call-start = ((), (), s32[]{:S(2)}) async-start(), calls=%async_computation.5 | async-start | bytes 1048576 | tf_op jit(solution)/shard_map/psum | solution.py:19
  1372.0 65.2 %copy-start.5 = (s32[2,64]{1,0:T(2,128)S(1)}, s32[2,64]{1,0:T(2,128)}, u32[]{:S(2)}) copy-start(s32[2,64]{1,0:T(2,128)} %param.13) | copy-start | bytes 1540
  1422.5 38.0 %copy-start.3 = (bf16[128,2048]{1,0:T(8,128)(2,1)S(1)}, bf16[128,2048]{1,0:T(8,128)(2,1)}, u32[]{:S(2)}) copy-start(bf16[128,2048]{1,0:T(8,128)(2,1)} %all-reduce.2.cloned.1.call-done) | copy-start | bytes 1572868
  1422.6 14.6 collective-permute-start.4
  1437.2 16.7 %collective-permute-start.5 = (bf16[128,2048]{1,0:T(8,128)(2,1)S(1)}, bf16[128,2048]{1,0:T(8,128)(2,1)S(1)}, u32[]{:S(2)}, u32[]{:S(2)}) collective-permute-start(bf16[128,2048]{1,0:T(8,128)(2,1)S(1)} %collective-permute-done.4), channel_id=1, source_target_pairs={{0,4},{4,8},{8,12},{12,0},{1,5},{5,9},{9,13},{13,1},{2,6},{6,10},{... | collective-permute-start | bytes 1572872 | tf_op jit(solution)/shard_map/ppermute | solution.py:78
  1437.2 23.1 %collective-permute-start.6 = (bf16[128,2048]{1,0:T(8,128)(2,1)}, bf16[128,2048]{1,0:T(8,128)(2,1)S(1)}, u32[]{:S(2)}, u32[]{:S(2)}) collective-permute-start(bf16[128,2048]{1,0:T(8,128)(2,1)} %all-reduce.2.cloned.1.call-done), channel_id=1, source_target_pairs={{0,12},{4,0},{8,4},{12,8},{1,13},{5,1},{9,5},{13,9},{2,14},{6,2},{... | collective-permute-start | bytes 1572872 | tf_op jit(solution)/shard_map/ppermute | solution.py:80
Sparse Core Ops, SparseCore 0:
  376.6 209.1 all-gather.20
  1175.0 32.3 all-gather.12
  1229.3 32.3 all-gather.14
  1283.7 32.3 all-gather.16
  1338.0 32.3 all-gather.18
  1389.8 32.7 all-reduce.1
